TPU v7x, 256 devices: a whole 4x4x8 slice. The times are simulated.
256 devices in a mesh: seq: 64 (over z_hi, y, x, core), head: 4 (over z_lo).
Axes of the slice: x: 4, y: 4, z: 8 (z_hi: 2, z_lo: 4; z = z_hi * 4 + z_lo), core: 2. Of those that a mesh axis runs over, the one named last changes fastest.
Arguments:
- queries: bfloat16 [64, 64, 192], P('seq', 'head'), may hold values from -120 to 120
- new_latent: bfloat16 [64, 576], P('seq'), may hold values from -6 to 6
- cache: bfloat16 [16, 8192, 576], P('head', 'seq'), may hold values from -6 to 6
- lengths: int32 [16], replicated, may hold values from 8 to 8192, as said below
- w_uk: bfloat16 [64, 128, 512], P('head'), may hold values from -0.5 to 0.5
- w_uv: bfloat16 [64, 512, 128], P('head'), may hold values from -0.25 to 0.25
Outputs:
- attended: bfloat16 [64, 64, 128], P('seq', 'head')
Inputs may be any that keep to these rules, and one draw needn't show every extreme that they name: `lengths`: each sequence keeps at least 8 cached slots; some sequence has exactly 8192.
All inputs are finite; a program needn't handle non-finite values.
Results may differ from a plain program's by a relative error of at most 0.039.
Values may be sent and summed in bfloat16 or wider, within the bound.
A program may use at most 64 MiB of HBM per device.

v0:
```python
import math

import jax
import jax.numpy as jnp
from jax import lax
from jax.sharding import PartitionSpec as P

NOPE = 128
ROPE = 64
LATENT = 512
SPEC = 4


masked_value = -1e30


def side_by_side(arrays, axis, dim, along):
    columns = [a.reshape(*a.shape[:along], -1) for a in arrays]
    both = jnp.concatenate(columns, axis=along)
    result, at, done = (lax.all_gather(both, axis, axis=dim, tiled=True), 0, [])
    for a, column in zip(arrays, columns):
        section = result[..., at : at + column.shape[along]]
        done.append(section.reshape(*section.shape[:along], *a.shape[along:]))
        at += column.shape[along]
    return tuple(done)


def copy_for_each(array, axis):
    count = lax.axis_size(axis)
    return lax.all_to_all(
        jnp.broadcast_to(array[None], (count, *array.shape)), axis, 0, 0, tiled=True
    )


def joined_along(parts, dim):
    shape = list(parts.shape[1:])
    shape[dim] *= parts.shape[0]
    return jnp.moveaxis(parts, 0, dim).reshape(shape)


def collect(array, axis, dim):
    parts = copy_for_each(array, axis)
    return joined_along(parts, dim)


def of_everyone(array, axis):
    everything = copy_for_each(array, axis)
    return jnp.max(everything, axis=0)


def split_up(array, dim, count):
    shape = array.shape
    parts = array.reshape(*shape[:dim], count, shape[dim] // count, *shape[dim + 1 :])
    return jnp.moveaxis(parts, dim, 0)


def sent_and_summed(array, axis, dim):
    count = lax.axis_size(axis)
    parts = lax.all_to_all(split_up(array, dim, count), axis, 0, 0, tiled=True)
    return jnp.sum(parts, axis=0)


def side_by_side_2(arrays, axis, dim, along):
    widths = [math.prod(a.shape[along:]) for a in arrays]
    both = jnp.concatenate(
        [a.reshape(*a.shape[:along], w) for a, w in zip(arrays, widths)], axis=along
    )
    result = sent_and_summed(both, axis, dim)
    parts = jnp.split(result, [sum(widths[:k]) for k in range(1, len(widths))], axis=along)
    return tuple(
        (b.reshape(*result.shape[:along], *a.shape[along:]) for a, b in zip(arrays, parts))
    )


def local_partial(
    query_tile_block,
    key_tile_block,
    incoming_keys,
    len_block,
    offset,
    own_first,
    score_scale,
    head_count,
):
    scores = (
        jnp.einsum(
            "vfa,vja->vfj", query_tile_block, key_tile_block, preferred_element_type=jnp.float32
        )
        * score_scale
    )
    positions = offset + lax.broadcasted_iota(jnp.int32, (1, 1, key_tile_block.shape[1]), 2)
    visible = positions < len_block[:, None, None]
    fresh_scores = (
        jnp.einsum(
            "vfa,vja->vfj", query_tile_block, incoming_keys, preferred_element_type=jnp.float32
        )
        * score_scale
    )
    spec_count = incoming_keys.shape[1]
    row_spec = (
        lax.broadcasted_iota(jnp.int32, (1, query_tile_block.shape[1], spec_count), 1) // head_count
    )
    key_spec = lax.broadcasted_iota(jnp.int32, (1, query_tile_block.shape[1], spec_count), 2)
    causal = (key_spec <= row_spec) & own_first
    row_top = jnp.maximum(
        jnp.max(jnp.where(visible, scores, masked_value), axis=2),
        jnp.max(jnp.where(causal, fresh_scores, masked_value), axis=2),
    )
    weights = jnp.where(visible, jnp.exp(scores - row_top[..., None]), 0.0)
    fresh_weights = jnp.where(causal, jnp.exp(fresh_scores - row_top[..., None]), 0.0)
    running_totals = jnp.sum(weights, axis=2) + jnp.sum(fresh_weights, axis=2)
    weighted = jnp.einsum(
        "mpu,mui->mpi",
        weights.astype(jnp.bfloat16),
        key_tile_block[:, :, :LATENT],
        preferred_element_type=jnp.float32,
    )
    weighted = weighted + jnp.einsum(
        "mpu,mui->mpi",
        fresh_weights.astype(jnp.bfloat16),
        incoming_keys[:, :, :LATENT],
        preferred_element_type=jnp.float32,
    )
    return (row_top, running_totals, weighted)


def project_values(latent_rows, value_weight):
    return jnp.einsum("rhc,hcv->rhv", latent_rows, value_weight, precision=lax.Precision.HIGHEST)


def shards(queries, new_latent, cache, lengths, w_uk, w_uv):
    own_rows, head_count, _ = queries.shape
    score_scale = (NOPE + ROPE) ** (-0.5)
    absorbed = jnp.einsum(
        "rhn,hnc->rhc", queries[:, :, :NOPE], w_uk, preferred_element_type=jnp.float32
    ).astype(jnp.bfloat16)
    outgoing = jnp.concatenate([absorbed, queries[:, :, NOPE:]], axis=2)
    gathered, new_all = side_by_side((outgoing, new_latent), "seq", 0, 1)
    total_rows = gathered.shape[0]
    seq_count = total_rows // SPEC
    query_slots = SPEC * head_count
    q_seq = gathered.reshape(seq_count, query_slots, gathered.shape[2])
    new_seq = new_all.reshape(seq_count, SPEC, new_all.shape[1])
    seq_index = lax.axis_index("seq")
    offset = seq_index * cache.shape[1]
    own_first = seq_index == 0
    partial_value = local_partial(
        q_seq,
        collect(cache, "head", 0),
        new_seq,
        lengths,
        offset,
        own_first,
        score_scale,
        head_count,
    )
    row_top, running_totals, weighted = tuple((value for value in partial_value))
    value_weight = w_uv.astype(jnp.float32)
    peak_top = of_everyone(row_top, "seq")
    factor = jnp.exp(row_top - peak_top)
    scaled_totals = (running_totals * factor).reshape(total_rows, head_count)
    scaled_weighted = (weighted * factor[..., None]).reshape(total_rows, head_count, LATENT)
    projected = project_values(scaled_weighted, value_weight)
    row_totals, row_projected = side_by_side_2((scaled_totals, projected), "seq", 0, 2)
    result = row_projected / row_totals[..., None]
    return result.astype(jnp.bfloat16)


def solution(mesh):
    return jax.shard_map(
        shards,
        mesh=mesh,
        in_specs=(
            P("seq", "head", None),
            P("seq", None),
            P("head", "seq", None),
            P(),
            P("head", None, None),
            P("head", None, None),
        ),
        out_specs=P("seq", "head", None),
        check_vma=False,
    )
```

profile of v0, /device:TPU:33, one launch (start us, length us, event | category | flops | bytes accessed | tf_op | source)
XLA Modules:
  0.0 201.4 jit_solution(1775720277473700367)
XLA Ops:
  6.5 0.0 copy-start
  6.5 3.1 %broadcast_in_dim.53 = bf16[4,4,128,576]{2,3,1,0:T(8,128)(2,1)} broadcast(bf16[4,128,576]{1,2,0:T(8,128)(2,1)} %param.8), dimensions={1,2,3} | broadcast | bytes 2949120 | tf_op jit(solution)/shard_map/broadcast_in_dim | solution.py:31
  9.7 0.0 copy-start.2
  9.7 5.6 %all-to-all-start = ((bf16[4,4,128,576]{2,3,1,0:T(8,128)(2,1)}), bf16[4,4,128,576]{2,3,1,0:T(8,128)(2,1)}, u32[]{:S(2)}, u32[]{:S(2)}) async-start(bf16[4,4,128,576]{2,3,1,0:T(8,128)(2,1)} %broadcast_in_dim.53), calls=%async_computation | async-start | bytes 4718592 | tf_op jit(solution)/shard_map/all_to_all | solution.py:30
  15.3 0.0 slice-start
  15.3 0.0 copy-start.3
  15.3 0.0 copy-start.4
  15.3 0.0 all-gather.3.cloned.1.call-start
  15.3 0.0 copy-done.2
  15.3 2.0 fusion.22
  17.3 0.0 slice-done
  17.3 0.1 reshape.175
  17.4 0.0 copy-done.3
  17.4 0.7 maximum_bitcast_fusion.1
  18.1 0.0 all-gather.3.cloned.1.call-update
  18.2 0.0 copy-done.4
  18.2 0.1 broadcast_compare_fusion
  18.3 97.1 %all-gather.3.cloned.1.call-done = bf16[64,1,9792]{2,1,0:T(2,128)(2,1)} async-done(((bf16[1,1,9792]{2,1,0:T(2,128)(2,1)}), bf16[64,1,9792]{2,1,0:T(2,128)(2,1)}) %all-gather.3.cloned.1.call-update) | async-done | bytes 1253392 | tf_op jit(solution)/shard_map/all_gather | solution.py:20
  115.3 1.9 copy.38
  117.2 1.1 slice.24
  118.3 0.6 slice.25
  118.9 2.2 %reshape_reshape.4 = bf16[16,64,576]{2,1,0:T(8,128)(2,1)S(1)} reshape(bf16[64,9216]{1,0:T(8,128)(2,1)} %slice.24) | data formatting | bytes 2359296 | tf_op jit(solution)/shard_map/reshape;reshape | solution.py:142
  121.2 0.9 reshape.177
  122.1 0.5 select_reduce_fusion.1
  122.6 0.0 all-to-all-done
  122.6 3.1 %select_reduce_fusion = (f32[16,64]{1,0:T(8,128)S(1)}, f32[16,64,128]{2,1,0:T(8,128)}) fusion(pred[16,128]{1,0:T(8,128)(4,1)S(1)} %broadcast_compare_fusion, bf16[16,64,576]{2,1,0:T(8,128)(2,1)S(1)} %reshape_reshape.4, bf16[16,128,576]{1,2,0:T(8,128)(2,1)} %bitcast.5), kind=kOutput, calls=%fused_computation.11 | convolution fusion | flops 151387136 | bytes 4069376 | tf_op jit(solution)/shard_map/vfa,vja->vfj/dot_general | solution.py:86
  125.7 0.0 copy-start.1
  125.8 1.0 reshape.185
  126.8 7.1 %all-to-all-start.1 = ((f32[64,1,1024]{2,1,0:T(1,128)}), f32[64,1,1024]{2,1,0:T(1,128)S(1)}, u32[]{:S(2)}, u32[]{:S(2)}) async-start(f32[64,1,1024]{2,1,0:T(1,128)} %reshape.185), calls=%async_computation.1 | async-start | bytes 524288 | tf_op jit(solution)/shard_map/all_to_all | solution.py:30
  133.9 0.0 copy-done.1
  133.9 0.4 fusion.8
  134.3 3.9 %fusion = f32[16,64,512]{2,1,0:T(8,128)} fusion(bf16[16,128,576]{1,2,0:T(8,128)(2,1)} %bitcast.5, f32[16,64,128]{2,1,0:T(8,128)S(1)} %copy-done.1, f32[16,64]{1,0:T(8,128)S(1)} %max.22, pred[16,128]{1,0:T(8,128)(4,1)S(1)} %broadcast_compare_fusion), kind=kOutput, calls=%fused_computation | convolution fusion | flops 134610944 | bytes 4724736 | tf_op jit(solution)/shard_map/mpu,mui->mpi/dot_general | solution.py:112
  138.2 11.6 %all-to-all-done.1 = f32[64,1,1024]{2,1,0:T(1,128)S(1)} async-done(((f32[64,1,1024]{2,1,0:T(1,128)}), f32[64,1,1024]{2,1,0:T(1,128)S(1)}, u32[]{:S(2)}, u32[]{:S(2)}) %all-to-all-start.1) | async-done | bytes 262176 | tf_op jit(solution)/shard_map/all_to_all | solution.py:30
  149.8 0.5 broadcast.83
  150.3 1.3 reduce.3
  151.6 0.1 reshape.186
  151.7 0.1 reduce_max.29
  151.8 0.1 mul.42
  151.9 0.6 copy.22
  152.5 2.1 %add_multiply_fusion = f32[16,64,512]{2,1,0:T(8,128)S(1)} fusion(f32[16,64,512]{2,1,0:T(8,128)} %fusion, f32[16,64]{1,0:T(8,128)S(1)} %get-tuple-element.6, bf16[16,4,576]{2,1,0:T(4,128)(2,1)S(1)} %reshape.177, f32[16,64,4]{1,2,0:T(4,128)S(1)} %get-tuple-element.10, f32[16,64]{1,0:T(8,128)S(1)} %max.22, pred[64,4]{0,1:T(4,128)(4,1)S(1)} %fusion.24), kind=kOutput, calls=%fused_computation.4 | convolution fusion | flops 5255168 | bytes 4309504 | tf_op jit(solution)/shard_map/mpu,mui->mpi/dot_general | solution.py:118
  154.6 0.0 copy-done
  154.6 2.3 %fusion.4 = f32[64,16,128]{2,0,1:T(8,128)S(1)} fusion(bf16[16,512,128]{2,1,0:T(8,128)(2,1)S(1)} %copy-done, f32[64,16,512]{2,1,0:T(8,128)S(1)} %bitcast.29), kind=kOutput, calls=%fused_computation.6 | convolution fusion | flops 805306368 | bytes 4718592 | tf_op jit(solution)/shard_map/rhc,hcv->rhv/dot_general | solution.py:128
  156.9 0.3 maximum_bitcast_fusion
  157.2 0.6 copy.23
  157.9 35.8 %all_to_all.15 = f32[64,1,16,129]{3,2,1,0:T(8,128)S(1)} all-to-all(f32[64,1,16,129]{3,2,1,0:T(8,128)S(1)} %copy.23), channel_id=1, replica_groups=mesh['seq'=64,'head'=4] {'seq'}, dimensions={0} | all-to-all | bytes 1056768 | tf_op jit(solution)/shard_map/all_to_all | solution.py:59
  193.6 0.1 reduce_sum.31
  193.7 0.1 slice_reduce_fusion
  193.9 0.7 fusion.21
  (11 shorter events, 0.1 us)
Async XLA Ops:
  6.5 148.1 %copy-start = (bf16[16,512,128]{2,1,0:T(8,128)(2,1)S(1)}, bf16[16,512,128]{2,1,0:T(8,128)(2,1)}, u32[]{:S(2)}) copy-start(bf16[16,512,128]{2,1,0:T(8,128)(2,1)} %param.11) | copy-start | bytes 6291460
  9.7 5.6 %copy-start.2 = (bf16[1,16,192]{2,1,0:T(8,128)(2,1)S(1)}, bf16[1,16,192]{2,1,0:T(8,128)(2,1)}, u32[]{:S(2)}) copy-start(bf16[1,16,192]{2,1,0:T(8,128)(2,1)} %param.6) | copy-start | bytes 18436
  9.7 112.9 %all-to-all-start = ((bf16[4,4,128,576]{2,3,1,0:T(8,128)(2,1)}), bf16[4,4,128,576]{2,3,1,0:T(8,128)(2,1)}, u32[]{:S(2)}, u32[]{:S(2)}) async-start(bf16[4,4,128,576]{2,3,1,0:T(8,128)(2,1)} %broadcast_in_dim.53), calls=%async_computation | async-start | bytes 4718592 | tf_op jit(solution)/shard_map/all_to_all | solution.py:30
  15.3 2.1 %slice-start = ((bf16[1,16,192]{2,1,0:T(8,128)(2,1)}), bf16[1,16,64]{2,1,0:T(8,128)(2,1)S(1)}, s32[]{:S(2)}) async-start(bf16[1,16,192]{2,1,0:T(8,128)(2,1)} %param.6), calls=%async_computation.4 | async-start | bytes 8192 | tf_op jit(solution)/shard_map/slice | solution.py:137
  15.3 2.2 %copy-start.3 = (bf16[1,576]{1,0:T(2,128)(2,1)S(1)}, bf16[1,576]{1,0:T(2,128)(2,1)}, u32[]{:S(2)}) copy-start(bf16[1,576]{1,0:T(2,128)(2,1)} %param.7) | copy-start | bytes 3460
  15.3 2.9 %copy-start.4 = (s32[16]{0:T(128)S(1)}, s32[16]{0:T(128)}, u32[]{:S(2)}) copy-start(s32[16]{0:T(128)} %param.9) | copy-start | bytes 196
  15.3 100.1 %all-gather.3.cloned.1.call-start = ((), (), s32[]{:S(2)}) async-start(), calls=%async_computation.3 | async-start | bytes 2562560 | tf_op jit(solution)/shard_map/all_gather | solution.py:20
  125.7 8.2 %copy-start.1 = (f32[16,64,128]{2,1,0:T(8,128)S(1)}, f32[16,64,128]{2,1,0:T(8,128)}, u32[]{:S(2)}) copy-start(f32[16,64,128]{2,1,0:T(8,128)} %get-tuple-element.8) | copy-start | bytes 1572868
  126.8 23.0 %all-to-all-start.1 = ((f32[64,1,1024]{2,1,0:T(1,128)}), f32[64,1,1024]{2,1,0:T(1,128)S(1)}, u32[]{:S(2)}, u32[]{:S(2)}) async-start(f32[64,1,1024]{2,1,0:T(1,128)} %reshape.185), calls=%async_computation.1 | async-start | bytes 524288 | tf_op jit(solution)/shard_map/all_to_all | solution.py:30
Sparse Core Ops, SparseCore 0:
  19.7 95.5 all-gather.2
where the time goes:
time: 202 us; the launch traced here: 201 us
  waiting for transfers between devices  109 us (54%)
  blocking collectives  35.8 us (18%)
  matrix products  13.8 us (7%)
  between operations  13.6 us (7%)
  local copies, waits for them, and re-layouts  13.1 us (6%)
  starting transfers between devices  12.7 us (6%)
  other arithmetic  3.7 us (2%)
    all_gather x1, waiting for transfers between devices, side_by_side(): result, at, done = (lax.all_gather(both, axis, axis=dim, tiled=True), 0, [])  97.1 us
    all_to_all x1, blocking collectives, sent_and_summed(): parts = lax.all_to_all(split_up(array, dim, count), axis, 0, 0, tiled=True)  35.8 us
    all_to_all x2, starting transfers between devices, copy_for_each(): lax.all_to_all(jnp.broadcast_to(array[None], (count, *array.shape)), axis...  12.6 us
    all_to_all x2, waiting for transfers between devices, copy_for_each(): lax.all_to_all(jnp.broadcast_to(array[None], (count, *array.shape)), axis...  11.6 us
  transfers between devices with their start and end apart: 3, of which 2 were waited for; matrix products, arithmetic and copies ran while one was open for 7% of the time, Pallas kernels for 0%

commit v1 on v0

v1 whole, which is shorter than its diff:
```python
import jax
import jax.numpy as jnp
from jax import lax
from jax.experimental import pallas as pl
from jax.experimental.pallas import tpu as pltpu
from jax.sharding import PartitionSpec as P

NOPE = 128
ROPE = 64
LATENT = 512
WIDTH = LATENT + ROPE
VDIM = 128
SPEC = 4
GROUP = 16
HEADS = 64
SLOTS = 128
NEG = -1e30
SCALE = (NOPE + ROPE) ** -0.5
MESH = pl.DeviceIdType.MESH
F32 = jnp.float32
BF16 = jnp.bfloat16


def dot(a, b, dims):
    return lax.dot_general(a, b, (dims, ((), ())), preferred_element_type=F32)


def kernel(
    q_hbm, nl_hbm, cache_hbm, len_ref, wuk_hbm, wuv_hbm, out_ref,
    wuk, wuv, q_in, nl, kt, kv, q_own, q_all, acc, o_out, s_out, o_in, s_in,
    r_out, t_out, r_in, t_in,
    local_sem, swap_send, swap_recv, nl_send, nl_recv, a_send, a_recv, b_send, b_recv,
    o_send, o_recv, s_send, s_recv, r_send, r_recv, t_send, t_recv,
):
    seq, head = lax.axis_index("seq"), lax.axis_index("head")
    core = lax.rem(seq, 2)
    x = lax.rem(lax.div(seq, 2), 4)
    y = lax.rem(lax.div(seq, 8), 4)
    zhi = lax.div(seq, 32)

    def at(zhi_, y_, x_, core_):
        return ((zhi_ * 4 + y_) * 4 + x_) * 2 + core_

    to_head, to_core = zhi * 2 + lax.div(y, 2), lax.rem(y, 2)
    plane = zhi * 4 + y
    from_zhi, from_y = lax.div(head, 2), lax.rem(head, 2) * 2 + core
    own_piece = (to_head == head) & (to_core == core)

    def worker(j):
        k = lax.rem(plane + j, 8)
        return (k * 4 + x) * 2 + to_core, to_head

    def owner(j):
        core_ = lax.rem(core + j // 4, 2)
        head_ = lax.rem(head + j % 4, 4)
        return at(from_zhi, from_y, x, core_), head_

    def x_peer(d):
        return at(zhi, y, lax.rem(x + d, 4), core), head

    mate_x = x + 1 - 2 * lax.rem(x, 2)
    mates = [
        (at(zhi, y, x, 1 - core), head),
        (at(zhi, y, mate_x, core), head),
        (at(zhi, y, mate_x, 1 - core), head),
    ]

    barrier = pltpu.get_barrier_semaphore()

    def greet(device):
        pl.semaphore_signal(barrier, inc=1, device_id=device, device_id_type=MESH)

    for j in range(1, 8):
        greet(worker(j))
        greet(owner(j))

    @pl.when(jnp.logical_not(own_piece))
    def _():
        greet(worker(0))
        greet(owner(0))

    for d in (1, 2, 3):
        greet(x_peer(d))
    greet(mates[0])
    greet(mates[2])

    def remote(src, dst, send, recv, device):
        return pltpu.make_async_remote_copy(
            src_ref=src, dst_ref=dst, send_sem=send, recv_sem=recv,
            device_id=device, device_id_type=MESH,
        )

    half = pl.ds(pl.multiple_of(core * SLOTS, SLOTS), SLOTS)
    token = lax.rem(seq, SPEC)

    load_q = pltpu.make_async_copy(q_hbm.at[0], q_in, local_sem.at[0])
    load_wuk = pltpu.make_async_copy(wuk_hbm, wuk, local_sem.at[1])
    load_nl = pltpu.make_async_copy(nl_hbm, nl.at[token], local_sem.at[2])
    load_kt = pltpu.make_async_copy(
        cache_hbm.at[pl.ds(2 * core, 2)], kt.at[:, :, half], local_sem.at[3]
    )
    load_wuv = pltpu.make_async_copy(wuv_hbm, wuv, local_sem.at[4])
    load_q.start()
    load_wuk.start()
    load_nl.start()
    load_kt.start()
    load_wuv.start()

    load_q.wait()
    q = q_in[...]
    row_of = lax.broadcasted_iota(jnp.int32, (GROUP, GROUP * NOPE), 0)
    col_of = lax.broadcasted_iota(jnp.int32, (GROUP, GROUP * NOPE), 1)
    spread = jnp.concatenate([q[:, :NOPE].astype(F32)] * GROUP, axis=1)
    spread = jnp.where(lax.div(col_of, NOPE) == row_of, spread, 0.0).astype(BF16)
    load_wuk.wait()
    absorbed = dot(spread, wuk[...], ((1,), (0,)))
    q_own[:, :LATENT] = absorbed.astype(BF16)
    q_own[:, LATENT:] = q[:, NOPE:]

    pl.semaphore_wait(barrier, jnp.where(own_piece, 19, 21))

    my_slot = core * 4 + head
    my_rows = pl.ds(pl.multiple_of(GROUP * head, GROUP), GROUP)
    my_place = q_all.at[2 * x + core, my_rows]
    for j in range(1, 8):
        remote(q_own, my_place, a_send.at[j], a_recv.at[my_slot], worker(j)).start()

    @pl.when(own_piece)
    def _():
        pltpu.make_async_copy(q_own, my_place, a_recv.at[my_slot]).start()

    @pl.when(jnp.logical_not(own_piece))
    def _():
        remote(q_own, my_place, a_send.at[0], a_recv.at[my_slot], worker(0)).start()

    swap = remote(
        cache_hbm.at[pl.ds(2 * (1 - core), 2)], kt.at[:, :, half],
        swap_send, swap_recv, mates[0],
    )
    swap.start()
    load_nl.wait()
    for k in range(3):
        remote(nl.at[token], nl.at[token], nl_send.at[k], nl_recv.at[token], mates[k]).start()

    load_kt.wait()
    other = pl.ds(pl.multiple_of((1 - core) * SLOTS, SLOTS), SLOTS)
    pltpu.make_async_copy(
        cache_hbm.at[pl.ds(0, 2)], kt.at[:, :, other], swap_recv
    ).wait()
    for s in range(2):
        kv[s] = kt[s].T

    x_rows = pl.ds(2 * x, 2)
    for c in range(2):
        core_ = lax.rem(core + c, 2)
        for g in range(4):
            head_ = lax.rem(head + g, 4)
            pltpu.make_async_copy(
                q_own,
                q_all.at[2 * x + core_, pl.ds(pl.multiple_of(GROUP * head_, GROUP), GROUP)],
                a_recv.at[core_ * 4 + head_],
            ).wait()
    for d in (1, 3, 2):
        remote(
            q_all.at[x_rows], q_all.at[x_rows], b_send.at[d], b_recv.at[d], x_peer(d)
        ).start()

    chip = lax.div(seq, 2)
    first = 4 * head + 2 * core

    def partial_of(x_, s):
        queries = q_all[pl.ds(2 * x_, 2)].reshape(2 * HEADS, WIDTH)
        scores = dot(kv[s], queries, ((1,), (1,))) * SCALE
        position = chip * (2 * SLOTS) + lax.broadcasted_iota(jnp.int32, scores.shape, 0)
        visible = position < len_ref[first + s]
        top = jnp.max(jnp.where(visible, scores, NEG), axis=0, keepdims=True)
        p = jnp.where(visible, jnp.exp(scores - top), 0.0)
        total = jnp.sum(p, axis=0, keepdims=True)
        weighted = dot(kt[s, :LATENT], p.astype(BF16), ((1,), (0,)))
        return top, total, weighted

    sub = lax.broadcasted_iota(jnp.int32, (8, 2 * HEADS), 0)

    def stats(top, total):
        return jnp.where(sub == 0, top, jnp.where(sub == 1, total, 0.0))

    top0, total0, weighted0 = partial_of(x, lax.div(x, 2))
    acc[...] = weighted0
    for d in (1, 3, 2):
        x_ = lax.rem(x + 4 - d, 4)
        rows = pl.ds(2 * x_, 2)
        pltpu.make_async_copy(q_all.at[rows], q_all.at[rows], b_recv.at[d]).wait()
        top, total, weighted = partial_of(x_, lax.div(x_, 2))
        o_out[d] = weighted.astype(BF16)
        s_out[d] = stats(top, total)
        remote(s_out.at[d], s_in.at[d], s_send.at[d], s_recv.at[d], x_peer(4 - d)).start()
        remote(o_out.at[d], o_in.at[d], o_send.at[d], o_recv.at[d], x_peer(4 - d)).start()

    for d in (1, 3, 2):
        pltpu.make_async_copy(s_in.at[d], s_in.at[d], s_recv.at[d]).wait()
        pltpu.make_async_copy(o_in.at[d], o_in.at[d], o_recv.at[d]).wait()
    tops = [top0] + [s_in[d][0:1] for d in (1, 2, 3)]
    top = jnp.maximum(jnp.maximum(tops[0], tops[1]), jnp.maximum(tops[2], tops[3]))
    factors = [jnp.exp(t - top) for t in tops]
    total = total0 * factors[0]
    merged = acc[...] * factors[0]
    for d in (1, 2, 3):
        total = total + s_in[d][1:2] * factors[d]
        merged = merged + o_in[d].astype(F32) * factors[d]
    t_out[...] = stats(top, total)
    r_out[...] = merged.T.astype(BF16)

    def piece(j):
        core_, head_ = lax.rem(core + j // 4, 2), lax.rem(head + j % 4, 4)
        start = pl.multiple_of(HEADS * core_ + GROUP * head_, GROUP)
        return r_out.at[pl.ds(start, GROUP)]

    def send_to_owner(j):
        return (
            remote(t_out, t_in.at[plane], t_send.at[j], t_recv.at[plane], owner(j)),
            remote(piece(j), r_in.at[plane], r_send.at[j], r_recv.at[plane], owner(j)),
        )

    for j in range(1, 8):
        a, b = send_to_owner(j)
        a.start()
        b.start()

    @pl.when(own_piece)
    def _():
        pltpu.make_async_copy(t_out, t_in.at[plane], t_recv.at[plane]).start()
        pltpu.make_async_copy(piece(0), r_in.at[plane], r_recv.at[plane]).start()

    @pl.when(jnp.logical_not(own_piece))
    def _():
        a, b = send_to_owner(0)
        a.start()
        b.start()

    for k in range(1, 4):
        other_token = lax.rem(token + k, SPEC)
        pltpu.make_async_copy(nl.at[token], nl.at[other_token], nl_recv.at[other_token]).wait()
    mine = q_own[...].astype(F32)
    fresh, keys = [], []
    for i in range(SPEC):
        key = nl[i].astype(F32)
        score = jnp.sum(mine * key, axis=1, keepdims=True) * SCALE
        fresh.append(jnp.where(i <= token, score, NEG))
        keys.append(key[:, :LATENT])
    f_top = jnp.maximum(jnp.maximum(fresh[0], fresh[1]), jnp.maximum(fresh[2], fresh[3]))
    f_total, f_weighted = 0.0, 0.0
    for i in range(SPEC):
        p = jnp.where(i <= token, jnp.exp(fresh[i] - f_top), 0.0)
        f_total = f_total + p
        f_weighted = f_weighted + p.astype(BF16).astype(F32) * keys[i]

    load_wuv.wait()
    for k in range(8):
        pltpu.make_async_copy(t_in.at[k], t_in.at[k], t_recv.at[k]).wait()
        pltpu.make_async_copy(r_in.at[k], r_in.at[k], r_recv.at[k]).wait()
    lane = lax.broadcasted_iota(jnp.int32, (GROUP, 2 * HEADS), 1)
    mine_lane = lane == (
        HEADS * core + GROUP * head + lax.broadcasted_iota(jnp.int32, (GROUP, 2 * HEADS), 0)
    )

    def column(row):
        return jnp.sum(jnp.where(mine_lane, row, 0.0), axis=1, keepdims=True)

    tops = [column(t_in[k][0:1]) for k in range(8)]
    top = f_top
    for t in tops:
        top = jnp.maximum(top, t)
    f_factor = jnp.exp(f_top - top)
    total = f_total * f_factor
    latent = f_weighted * f_factor
    for k in range(8):
        factor = jnp.exp(tops[k] - top)
        total = total + column(t_in[k][1:2]) * factor
        latent = latent + r_in[k].astype(F32) * factor
    latent = latent / total

    high = latent.astype(BF16).astype(F32)
    both = jnp.concatenate([high, latent - high], axis=0)
    wide = jnp.concatenate([both] * GROUP, axis=1)
    row_of = lax.rem(lax.broadcasted_iota(jnp.int32, wide.shape, 0), GROUP)
    col_of = lax.div(lax.broadcasted_iota(jnp.int32, wide.shape, 1), LATENT)
    wide = jnp.where(row_of == col_of, wide, 0.0).astype(BF16)
    projected = dot(wide, wuv[...], ((1,), (0,)))
    out_ref[0] = (projected[:GROUP] + projected[GROUP:]).astype(BF16)

    for j in range(1, 8):
        remote(q_own, my_place, a_send.at[j], a_recv.at[my_slot], worker(j)).wait_send()
        a, b = send_to_owner(j)
        a.wait_send()
        b.wait_send()

    @pl.when(jnp.logical_not(own_piece))
    def _():
        remote(q_own, my_place, a_send.at[0], a_recv.at[my_slot], worker(0)).wait_send()
        a, b = send_to_owner(0)
        a.wait_send()
        b.wait_send()

    swap.wait_send()
    for k in range(3):
        remote(
            nl.at[token], nl.at[token], nl_send.at[k], nl_recv.at[token], mates[k]
        ).wait_send()
    for d in (1, 2, 3):
        remote(
            q_all.at[x_rows], q_all.at[x_rows], b_send.at[d], b_recv.at[d], x_peer(d)
        ).wait_send()
        remote(s_out.at[d], s_in.at[d], s_send.at[d], s_recv.at[d], x_peer(4 - d)).wait_send()
        remote(o_out.at[d], o_in.at[d], o_send.at[d], o_recv.at[d], x_peer(4 - d)).wait_send()


def shards(queries, new_latent, cache, lengths, w_uk, w_uv):
    anywhere = pl.BlockSpec(memory_space=pl.ANY)
    dma = pltpu.SemaphoreType.DMA
    return pl.pallas_call(
        kernel,
        out_shape=jax.ShapeDtypeStruct((1, GROUP, VDIM), BF16),
        in_specs=[
            anywhere,
            anywhere,
            anywhere,
            pl.BlockSpec(memory_space=pltpu.SMEM),
            anywhere,
            anywhere,
        ],
        out_specs=pl.BlockSpec(memory_space=pltpu.VMEM),
        scratch_shapes=[
            pltpu.VMEM((GROUP * NOPE, LATENT), BF16),
            pltpu.VMEM((GROUP * LATENT, VDIM), BF16),
            pltpu.VMEM((GROUP, NOPE + ROPE), BF16),
            pltpu.VMEM((SPEC, 1, WIDTH), BF16),
            pltpu.VMEM((2, WIDTH, 2 * SLOTS), BF16),
            pltpu.VMEM((2, 2 * SLOTS, WIDTH), BF16),
            pltpu.VMEM((GROUP, WIDTH), BF16),
            pltpu.VMEM((8, HEADS, WIDTH), BF16),
            pltpu.VMEM((LATENT, 2 * HEADS), F32),
            pltpu.VMEM((4, LATENT, 2 * HEADS), BF16),
            pltpu.VMEM((4, 8, 2 * HEADS), F32),
            pltpu.VMEM((4, LATENT, 2 * HEADS), BF16),
            pltpu.VMEM((4, 8, 2 * HEADS), F32),
            pltpu.VMEM((2 * HEADS, LATENT), BF16),
            pltpu.VMEM((8, 2 * HEADS), F32),
            pltpu.VMEM((8, GROUP, LATENT), BF16),
            pltpu.VMEM((8, 8, 2 * HEADS), F32),
            dma((5,)),
            dma,
            dma,
            dma((3,)),
            dma((4,)),
            dma((8,)),
            dma((8,)),
            dma((4,)),
            dma((4,)),
            dma((4,)),
            dma((4,)),
            dma((4,)),
            dma((4,)),
            dma((8,)),
            dma((8,)),
            dma((8,)),
            dma((8,)),
        ],
        compiler_params=pltpu.CompilerParams(
            collective_id=0, has_side_effects=True, vmem_limit_bytes=67_043_328
        ),
    )(
        queries,
        new_latent,
        jnp.swapaxes(cache, 1, 2),
        lengths,
        w_uk.reshape(GROUP * NOPE, LATENT),
        w_uv.reshape(GROUP * LATENT, VDIM),
    )


def solution(mesh):
    return jax.shard_map(
        shards,
        mesh=mesh,
        in_specs=(
            P("seq", "head", None),
            P("seq", None),
            P("head", "seq", None),
            P(),
            P("head", None, None),
            P("head", None, None),
        ),
        out_specs=P("seq", "head", None),
        check_vma=False,
    )
```

time: 202 us -> 49 us (0.24)
  the two profiles are of different devices: /device:TPU:33 before, /device:TPU:1 now
where the time goes in v1:
time: 49 us; the launch traced here: 48.8 us
  Pallas kernels  47.5 us (97%)
  local copies, waits for them, and re-layouts  1.28 us (3%)
    pallas_call x1, Pallas kernels, shards(): pl.pallas_call(kernel, out_shape=jax.ShapeDtypeStruct((1, GROUP, VDIM), B...  47.5 us
    unnamed x1, local copies, waits for them, and re-layouts  1.28 us

profile of v1, /device:TPU:1, one launch (start us, length us, event | category | flops | bytes accessed | tf_op | source)
XLA Modules:
  0.0 48.8 jit_solution(14224970590109314552)
XLA Ops:
  0.0 47.5 %shard_map.64 = bf16[1,16,128]{2,1,0:T(8,128)(2,1)} custom-call(bf16[1,16,192]{2,1,0:T(8,128)(2,1)} %q_hbm.1, bf16[1,576]{1,0:T(2,128)(2,1)} %nl_hbm.1, bf16[4,576,128]{2,1,0:T(8,128)(2,1)} %bitcast.5, s32[16]{0:T(128)} %len_ref.1, bf16[2048,512]{1,0:T(8,128)(2,1)} %bitcast.3, bf16[8192,128]{1,0:T(8,128)(2,1)} %bitcast.4), custom_call_target="tpu_custom_call" | custom-call | tf_op jit(solution)/shard_map/pallas_call | solution.py:320
  47.5 1.3 %copy.8 = bf16[1,16,128]{2,1,0:T(8,128)(2,1)} copy(bf16[1,16,128]{2,1,0:T(8,128)(2,1)} %shard_map.64) | data formatting | bytes 8192

commit v2 on v1

v2 whole, which is shorter than its diff:
```python
import jax
import jax.numpy as jnp
from jax import lax
from jax.experimental import pallas as pl
from jax.experimental.pallas import tpu as pltpu
from jax.sharding import PartitionSpec as P

NOPE = 128
ROPE = 64
LATENT = 512
WIDTH = LATENT + ROPE
VDIM = 128
SPEC = 4
GROUP = 16
HEADS = 64
SLOTS = 128
NEG = -1e30
SCALE = (NOPE + ROPE) ** -0.5
MESH = pl.DeviceIdType.MESH
F32 = jnp.float32
BF16 = jnp.bfloat16


def dot(a, b, dims):
    return lax.dot_general(a, b, (dims, ((), ())), preferred_element_type=F32)


def kernel(
    q_hbm, nl_hbm, cache_hbm, len_ref, wuk_hbm, wuv_hbm, out_ref,
    wuk, wuv, q_in, nl, kt, kv, q_own, q_all, o_out, s_out, o_in, s_in,
    r_out, t_out, r_in, t_in,
    local_sem, swap_send, swap_recv, nl_send, nl_recv, a_send, a_recv, b_send, b_recv,
    o_send, o_recv, s_send, s_recv, r_send, r_recv, t_send, t_recv, ready_a, ready_r,
):
    seq, head = lax.axis_index("seq"), lax.axis_index("head")
    core = lax.rem(seq, 2)
    x = lax.rem(lax.div(seq, 2), 4)
    y = lax.rem(lax.div(seq, 8), 4)
    zhi = lax.div(seq, 32)

    def at(zhi_, y_, x_, core_):
        return ((zhi_ * 4 + y_) * 4 + x_) * 2 + core_

    to_head, to_core = zhi * 2 + lax.div(y, 2), lax.rem(y, 2)
    plane = zhi * 4 + y
    from_zhi, from_y = lax.div(head, 2), lax.rem(head, 2) * 2 + core
    own_piece = (to_head == head) & (to_core == core)
    others_piece = jnp.logical_not(own_piece)

    def worker(j):
        zhi_ = zhi if j < 4 else 1 - zhi
        return at(zhi_, lax.rem(y + j % 4, 4), x, to_core), to_head

    def owner(j):
        return at(from_zhi, from_y, x, lax.rem(core + j // 4, 2)), lax.rem(head + j % 4, 4)

    odd = lax.rem(x, 2)
    near_x, pair_x, upper = x + 1 - 2 * odd, 3 - x, lax.div(x, 2)
    twin = (at(zhi, y, x, 1 - core), head)
    beside = (at(zhi, y, near_x, core), head)
    mates = [twin, beside, (at(zhi, y, near_x, 1 - core), head)]
    pair = [(at(zhi, y, pair_x, core), head), (at(zhi, y, pair_x, 1 - core), head)]

    barrier = pltpu.get_barrier_semaphore()

    def greet(device):
        pl.semaphore_signal(barrier, inc=1, device_id=device, device_id_type=MESH)

    def answer(sem, device):
        pl.semaphore_signal(sem, inc=1, device_id=device, device_id_type=MESH)

    for device in mates + pair:
        greet(device)
    for j in range(1, 4):
        greet(worker(j))

    @pl.when(others_piece)
    def _():
        greet(worker(0))

    @pl.when(zhi == 0)
    def _():
        for j in range(4, 8):
            greet(worker(j))

    @pl.when((zhi == 0) | (from_zhi == zhi))
    def _():
        for j in range(1, 8):
            greet(owner(j))

        @pl.when(others_piece)
        def _():
            greet(owner(0))

    greeted = 9 + 4 * zhi + jnp.where((zhi == 1) | (from_zhi == zhi), 8, 0)
    greeted = greeted - jnp.where(own_piece, 2, 0)

    def remote(src, dst, send, recv, device):
        return pltpu.make_async_remote_copy(
            src_ref=src, dst_ref=dst, send_sem=send, recv_sem=recv,
            device_id=device, device_id_type=MESH,
        )

    def slots(block):
        return kt.at[:, pl.ds(pl.multiple_of(block * SLOTS, SLOTS), SLOTS)]

    token = lax.rem(seq, SPEC)

    load_q = pltpu.make_async_copy(q_hbm.at[0], q_in, local_sem.at[0])
    load_wuk = pltpu.make_async_copy(wuk_hbm, wuk, local_sem.at[1])
    load_nl = pltpu.make_async_copy(nl_hbm, nl.at[token], local_sem.at[2])
    load_kt = pltpu.make_async_copy(
        cache_hbm.at[2 * core + upper], slots(core), local_sem.at[3]
    )
    load_wuv = pltpu.make_async_copy(wuv_hbm, wuv, local_sem.at[4])
    load_q.start()
    load_wuk.start()
    load_nl.start()
    load_kt.start()
    load_wuv.start()

    load_q.wait()
    q = q_in[...]
    row_of = lax.broadcasted_iota(jnp.int32, (GROUP, GROUP * NOPE), 0)
    col_of = lax.broadcasted_iota(jnp.int32, (GROUP, GROUP * NOPE), 1)
    spread = jnp.concatenate([q[:, :NOPE].astype(F32)] * GROUP, axis=1)
    spread = jnp.where(lax.div(col_of, NOPE) == row_of, spread, 0.0).astype(BF16)
    load_wuk.wait()
    absorbed = dot(spread, wuk[...], ((1,), (0,)))
    q_own[:, :LATENT] = absorbed.astype(BF16)
    q_own[:, LATENT:] = q[:, NOPE:]

    pl.semaphore_wait(barrier, greeted)

    my_slot = core * 4 + head

    def rows_of(x_, core_, head_):
        start = pl.multiple_of(GROUP * head_, GROUP)
        return q_all.at[2 * lax.rem(x_, 2) + core_, pl.ds(start, GROUP)]

    my_place = rows_of(x, core, head)

    def send_queries(j):
        return remote(q_own, my_place, a_send.at[j], a_recv.at[my_slot], worker(j))

    for j in range(1, 4):
        send_queries(j).start()

    @pl.when(own_piece)
    def _():
        pltpu.make_async_copy(q_own, my_place, a_recv.at[my_slot]).start()

    @pl.when(others_piece)
    def _():
        send_queries(0).start()

    swaps = [
        remote(cache_hbm.at[2 * (1 - core) + upper], slots(core),
               swap_send.at[0], swap_recv.at[core], twin),
        remote(cache_hbm.at[2 * core + 1 - upper], slots(2 + core),
               swap_send.at[1], swap_recv.at[2 + core], pair[0]),
        remote(cache_hbm.at[2 * (1 - core) + 1 - upper], slots(2 + core),
               swap_send.at[2], swap_recv.at[2 + core], pair[1]),
    ]
    load_nl.wait()
    news = [
        remote(nl.at[token], nl.at[token], nl_send.at[k], nl_recv.at[token], mates[k])
        for k in range(3)
    ]

    @pl.when(zhi == 1)
    def _():
        for j in range(4, 8):
            answer(ready_r, worker(j))

        @pl.when(from_zhi == 0)
        def _():
            for j in range(8):
                answer(ready_a, owner(j))

    for copy in swaps + news:
        copy.start()

    @pl.when(zhi == 0)
    def _():
        pl.semaphore_wait(ready_a, 4)

    for j in range(4, 8):
        send_queries(j).start()

    load_kt.wait()
    for block in (1 - core, 2, 3):
        pltpu.make_async_copy(cache_hbm.at[0], slots(block), swap_recv.at[block]).wait()
    kv[...] = kt[...].T

    def forward(c, g):
        place = rows_of(x, c, g)
        return remote(place, place, b_send.at[4 * c + g], b_recv.at[4 * c + g], beside)

    for g in range(4):
        for c in range(2):
            pltpu.make_async_copy(q_own, rows_of(x, c, g), a_recv.at[4 * c + g]).wait()
            forward(c, g).start()

    chip = lax.div(seq, 2)
    length = len_ref[4 * head + 2 * core + upper]
    step = (3 - 2 * x) * (2 * SLOTS)

    def partial_of(x_):
        queries = q_all[pl.ds(2 * lax.rem(x_, 2), 2)].reshape(2 * HEADS, WIDTH)
        scores = dot(kv[...], queries, ((1,), (1,))) * SCALE
        slot = lax.broadcasted_iota(jnp.int32, scores.shape, 0)
        position = chip * (2 * SLOTS) + jnp.where(
            slot < 2 * SLOTS, slot, slot - 2 * SLOTS + step
        )
        visible = position < length
        top = jnp.max(jnp.where(visible, scores, NEG), axis=0, keepdims=True)
        p = jnp.where(visible, jnp.exp(scores - top), 0.0)
        total = jnp.sum(p, axis=0, keepdims=True)
        weighted = dot(kt[:LATENT], p.astype(BF16), ((1,), (0,)))
        return top, total, weighted

    def put_stats(ref, top, total):
        ref[0:1] = top
        ref[1:2] = total

    top_0, total_0, weighted_0 = partial_of(x)
    for g in range(4):
        for c in range(2):
            pltpu.make_async_copy(q_own, rows_of(near_x, c, g), b_recv.at[4 * c + g]).wait()
    top_1, total_1, weighted_1 = partial_of(near_x)
    o_out[...] = weighted_1.astype(BF16)
    put_stats(s_out, top_1, total_1)
    back = [
        remote(s_out, s_in, s_send, s_recv, beside),
        remote(o_out, o_in, o_send, o_recv, beside),
    ]
    for copy in back:
        copy.start()

    for copy in back:
        copy.wait_recv()
    top_1, total_1 = s_in[0:1], s_in[1:2]
    top = jnp.maximum(top_0, top_1)
    factor_0, factor_1 = jnp.exp(top_0 - top), jnp.exp(top_1 - top)
    put_stats(t_out, top, total_0 * factor_0 + total_1 * factor_1)
    merged = weighted_0 * factor_0 + o_in[...].astype(F32) * factor_1
    r_out[...] = merged.T.astype(BF16)

    def piece(j):
        core_, head_ = lax.rem(core + j // 4, 2), lax.rem(head + j % 4, 4)
        start = pl.multiple_of(HEADS * core_ + GROUP * head_, GROUP)
        return r_out.at[pl.ds(start, GROUP)]

    def send_to_owner(j):
        return (
            remote(t_out, t_in.at[plane], t_send.at[j], t_recv.at[plane], owner(j)),
            remote(piece(j), r_in.at[plane], r_send.at[j], r_recv.at[plane], owner(j)),
        )

    @pl.when((zhi == 0) & (from_zhi == 1))
    def _():
        pl.semaphore_wait(ready_r, 8)

    for j in range(1, 8):
        for copy in send_to_owner(j):
            copy.start()

    @pl.when(own_piece)
    def _():
        pltpu.make_async_copy(t_out, t_in.at[plane], t_recv.at[plane]).start()
        pltpu.make_async_copy(piece(0), r_in.at[plane], r_recv.at[plane]).start()

    @pl.when(others_piece)
    def _():
        for copy in send_to_owner(0):
            copy.start()

    for k in range(1, 4):
        other_token = lax.rem(token + k, SPEC)
        pltpu.make_async_copy(nl.at[token], nl.at[other_token], nl_recv.at[other_token]).wait()
    mine = q_own[...].astype(F32)
    fresh, keys = [], []
    for i in range(SPEC):
        key = nl[i].astype(F32)
        score = jnp.sum(mine * key, axis=1, keepdims=True) * SCALE
        fresh.append(jnp.where(i <= token, score, NEG))
        keys.append(key[:, :LATENT])
    f_top = jnp.maximum(jnp.maximum(fresh[0], fresh[1]), jnp.maximum(fresh[2], fresh[3]))
    f_total, f_weighted = 0.0, 0.0
    for i in range(SPEC):
        p = jnp.where(i <= token, jnp.exp(fresh[i] - f_top), 0.0)
        f_total = f_total + p
        f_weighted = f_weighted + p.astype(BF16).astype(F32) * keys[i]
    load_wuv.wait()

    for k in range(8):
        pltpu.make_async_copy(t_in.at[k], t_in.at[k], t_recv.at[k]).wait()
        pltpu.make_async_copy(r_in.at[k], r_in.at[k], r_recv.at[k]).wait()
    lane = lax.broadcasted_iota(jnp.int32, (GROUP, 2 * HEADS), 1)
    mine_lane = lane == (
        HEADS * core + GROUP * head + lax.broadcasted_iota(jnp.int32, (GROUP, 2 * HEADS), 0)
    )

    def column(row):
        return jnp.sum(jnp.where(mine_lane, row, 0.0), axis=1, keepdims=True)

    tops = [column(t_in[k, 0:1]) for k in range(8)]
    top = f_top
    for t in tops:
        top = jnp.maximum(top, t)
    f_factor = jnp.exp(f_top - top)
    total = f_total * f_factor
    latent = f_weighted * f_factor
    for k in range(8):
        factor = jnp.exp(tops[k] - top)
        total = total + column(t_in[k, 1:2]) * factor
        latent = latent + r_in[k].astype(F32) * factor
    latent = latent / total

    high = latent.astype(BF16).astype(F32)
    both = jnp.concatenate([high, latent - high], axis=0)
    wide = jnp.concatenate([both] * GROUP, axis=1)
    row_of = lax.rem(lax.broadcasted_iota(jnp.int32, wide.shape, 0), GROUP)
    col_of = lax.div(lax.broadcasted_iota(jnp.int32, wide.shape, 1), LATENT)
    wide = jnp.where(row_of == col_of, wide, 0.0).astype(BF16)
    projected = dot(wide, wuv[...], ((1,), (0,)))
    out_ref[0] = (projected[:GROUP] + projected[GROUP:]).astype(BF16)

    for j in range(1, 8):
        send_queries(j).wait_send()
        for copy in send_to_owner(j):
            copy.wait_send()

    @pl.when(others_piece)
    def _():
        send_queries(0).wait_send()
        for copy in send_to_owner(0):
            copy.wait_send()

    for g in range(4):
        for c in range(2):
            forward(c, g).wait_send()
    for copy in swaps + news + back:
        copy.wait_send()


def shards(queries, new_latent, cache, lengths, w_uk, w_uv):
    anywhere = pl.BlockSpec(memory_space=pl.ANY)
    dma = pltpu.SemaphoreType.DMA
    return pl.pallas_call(
        kernel,
        out_shape=jax.ShapeDtypeStruct((1, GROUP, VDIM), BF16),
        in_specs=[
            anywhere,
            anywhere,
            anywhere,
            pl.BlockSpec(memory_space=pltpu.SMEM),
            anywhere,
            anywhere,
        ],
        out_specs=pl.BlockSpec(memory_space=pltpu.VMEM),
        scratch_shapes=[
            pltpu.VMEM((GROUP * NOPE, LATENT), BF16),
            pltpu.VMEM((GROUP * LATENT, VDIM), BF16),
            pltpu.VMEM((GROUP, NOPE + ROPE), BF16),
            pltpu.VMEM((SPEC, 1, WIDTH), BF16),
            pltpu.VMEM((WIDTH, 4 * SLOTS), BF16),
            pltpu.VMEM((4 * SLOTS, WIDTH), BF16),
            pltpu.VMEM((GROUP, WIDTH), BF16),
            pltpu.VMEM((4, HEADS, WIDTH), BF16),
            pltpu.VMEM((LATENT, 2 * HEADS), BF16),
            pltpu.VMEM((2, 2 * HEADS), F32),
            pltpu.VMEM((LATENT, 2 * HEADS), BF16),
            pltpu.VMEM((2, 2 * HEADS), F32),
            pltpu.VMEM((2 * HEADS, LATENT), BF16),
            pltpu.VMEM((2, 2 * HEADS), F32),
            pltpu.VMEM((8, GROUP, LATENT), BF16),
            pltpu.VMEM((8, 2, 2 * HEADS), F32),
            dma((5,)),
            dma((3,)),
            dma((4,)),
            dma((3,)),
            dma((4,)),
            dma((8,)),
            dma((8,)),
            dma((8,)),
            dma((8,)),
            dma,
            dma,
            dma,
            dma,
            dma((8,)),
            dma((8,)),
            dma((8,)),
            dma((8,)),
            pltpu.SemaphoreType.REGULAR,
            pltpu.SemaphoreType.REGULAR,
        ],
        compiler_params=pltpu.CompilerParams(
            collective_id=0, has_side_effects=True, vmem_limit_bytes=67_043_328
        ),
    )(
        queries,
        new_latent,
        jnp.swapaxes(cache, 1, 2),
        lengths,
        w_uk.reshape(GROUP * NOPE, LATENT),
        w_uv.reshape(GROUP * LATENT, VDIM),
    )


def solution(mesh):
    return jax.shard_map(
        shards,
        mesh=mesh,
        in_specs=(
            P("seq", "head", None),
            P("seq", None),
            P("head", "seq", None),
            P(),
            P("head", None, None),
            P("head", None, None),
        ),
        out_specs=P("seq", "head", None),
        check_vma=False,
    )
```

time: 49 us -> 41.8 us (0.85)
  Pallas kernels: 47.5 us -> 40.3 us
    pallas_call x1, Pallas kernels: 47.5 us -> 40.3 us  [shards(): pl.pallas_call(kernel, out_shape=jax.ShapeDtypeStruct((1, GROUP, VDIM), B...]
where the time goes in v2:
time: 41.8 us; the launch traced here: 41.6 us
  Pallas kernels  40.3 us (96%)
  local copies, waits for them, and re-layouts  1.28 us (3%)
    pallas_call x1, Pallas kernels, shards(): pl.pallas_call(kernel, out_shape=jax.ShapeDtypeStruct((1, GROUP, VDIM), B...  40.3 us
    unnamed x1, local copies, waits for them, and re-layouts  1.28 us

profile of v2, /device:TPU:1, one launch (start us, length us, event | category | flops | bytes accessed | tf_op | source)
XLA Modules:
  0.0 41.6 jit_solution(4963873511303275377)
XLA Ops:
  0.0 40.3 %shard_map.64 = bf16[1,16,128]{2,1,0:T(8,128)(2,1)} custom-call(bf16[1,16,192]{2,1,0:T(8,128)(2,1)} %q_hbm.1, bf16[1,576]{1,0:T(2,128)(2,1)} %nl_hbm.1, bf16[4,576,128]{2,1,0:T(8,128)(2,1)} %bitcast.5, s32[16]{0:T(128)} %len_ref.1, bf16[2048,512]{1,0:T(8,128)(2,1)} %bitcast.3, bf16[8192,128]{1,0:T(8,128)(2,1)} %bitcast.4), custom_call_target="tpu_custom_call" | custom-call | tf_op jit(solution)/shard_map/pallas_call | solution.py:351
  40.3 1.3 %copy.8 = bf16[1,16,128]{2,1,0:T(8,128)(2,1)} copy(bf16[1,16,128]{2,1,0:T(8,128)(2,1)} %shard_map.64) | data formatting | bytes 8192

commit v3 on v2

--- a/solution.py
+++ b/solution.py
@@ -13,6 +13,7 @@
 SPEC = 4
 GROUP = 16
 HEADS = 64
+SEQS = 16
 SLOTS = 128
 NEG = -1e30
 SCALE = (NOPE + ROPE) ** -0.5
@@ -26,11 +27,11 @@
 
 
 def kernel(
-    q_hbm, nl_hbm, cache_hbm, len_ref, wuk_hbm, wuv_hbm, out_ref,
-    wuk, wuv, q_in, nl, kt, kv, q_own, q_all, o_out, s_out, o_in, s_in,
+    q_hbm, nl_hbm, cache_hbm, len_hbm, wuk_hbm, wuv_hbm, out_ref,
+    len_ref, wuk, wuv, q_in, nl, kt, kv, q_own, q_all, o_out, s_out, o_in, s_in,
     r_out, t_out, r_in, t_in,
     local_sem, swap_send, swap_recv, nl_send, nl_recv, a_send, a_recv, b_send, b_recv,
-    o_send, o_recv, s_send, s_recv, r_send, r_recv, t_send, t_recv, ready_a, ready_r,
+    o_send, o_recv, s_send, s_recv, r_send, r_recv, t_send, t_recv,
 ):
     seq, head = lax.axis_index("seq"), lax.axis_index("head")
     core = lax.rem(seq, 2)
@@ -66,34 +67,17 @@
     def greet(device):
         pl.semaphore_signal(barrier, inc=1, device_id=device, device_id_type=MESH)
 
-    def answer(sem, device):
-        pl.semaphore_signal(sem, inc=1, device_id=device, device_id_type=MESH)
+    for j in range(7, 0, -1):
+        greet(worker(j))
+        greet(owner(j))
+
+    @pl.when(others_piece)
+    def _():
+        greet(worker(0))
+        greet(owner(0))
 
     for device in mates + pair:
         greet(device)
-    for j in range(1, 4):
-        greet(worker(j))
-
-    @pl.when(others_piece)
-    def _():
-        greet(worker(0))
-
-    @pl.when(zhi == 0)
-    def _():
-        for j in range(4, 8):
-            greet(worker(j))
-
-    @pl.when((zhi == 0) | (from_zhi == zhi))
-    def _():
-        for j in range(1, 8):
-            greet(owner(j))
-
-        @pl.when(others_piece)
-        def _():
-            greet(owner(0))
-
-    greeted = 9 + 4 * zhi + jnp.where((zhi == 1) | (from_zhi == zhi), 8, 0)
-    greeted = greeted - jnp.where(own_piece, 2, 0)
 
     def remote(src, dst, send, recv, device):
         return pltpu.make_async_remote_copy(
@@ -118,6 +102,8 @@
     load_nl.start()
     load_kt.start()
     load_wuv.start()
+    load_len = pltpu.make_async_copy(len_hbm, len_ref, local_sem.at[5])
+    load_len.start()
 
     load_q.wait()
     q = q_in[...]
@@ -130,7 +116,7 @@
     q_own[:, :LATENT] = absorbed.astype(BF16)
     q_own[:, LATENT:] = q[:, NOPE:]
 
-    pl.semaphore_wait(barrier, greeted)
+    pl.semaphore_wait(barrier, jnp.where(own_piece, 19, 21))
 
     my_slot = core * 4 + head
 
@@ -143,7 +129,7 @@
     def send_queries(j):
         return remote(q_own, my_place, a_send.at[j], a_recv.at[my_slot], worker(j))
 
-    for j in range(1, 4):
+    for j in (4, 5, 7, 6, 1, 3, 2):
         send_queries(j).start()
 
     @pl.when(own_piece)
@@ -168,41 +154,25 @@
         for k in range(3)
     ]
 
-    @pl.when(zhi == 1)
-    def _():
-        for j in range(4, 8):
-            answer(ready_r, worker(j))
-
-        @pl.when(from_zhi == 0)
-        def _():
-            for j in range(8):
-                answer(ready_a, owner(j))
-
     for copy in swaps + news:
         copy.start()
 
-    @pl.when(zhi == 0)
-    def _():
-        pl.semaphore_wait(ready_a, 4)
-
-    for j in range(4, 8):
-        send_queries(j).start()
+    def forward(c, g):
+        place = rows_of(x, c, g)
+        return remote(place, place, b_send.at[4 * c + g], b_recv.at[4 * c + g], beside)
+
+    for g in range(4):
+        for c in range(2):
+            pltpu.make_async_copy(q_own, rows_of(x, c, g), a_recv.at[4 * c + g]).wait()
+            forward(c, g).start()
 
     load_kt.wait()
     for block in (1 - core, 2, 3):
         pltpu.make_async_copy(cache_hbm.at[0], slots(block), swap_recv.at[block]).wait()
     kv[...] = kt[...].T
 
-    def forward(c, g):
-        place = rows_of(x, c, g)
-        return remote(place, place, b_send.at[4 * c + g], b_recv.at[4 * c + g], beside)
-
-    for g in range(4):
-        for c in range(2):
-            pltpu.make_async_copy(q_own, rows_of(x, c, g), a_recv.at[4 * c + g]).wait()
-            forward(c, g).start()
-
     chip = lax.div(seq, 2)
+    load_len.wait()
     length = len_ref[4 * head + 2 * core + upper]
     step = (3 - 2 * x) * (2 * SLOTS)
 
@@ -257,10 +227,6 @@
             remote(t_out, t_in.at[plane], t_send.at[j], t_recv.at[plane], owner(j)),
             remote(piece(j), r_in.at[plane], r_send.at[j], r_recv.at[plane], owner(j)),
         )
-
-    @pl.when((zhi == 0) & (from_zhi == 1))
-    def _():
-        pl.semaphore_wait(ready_r, 8)
 
     for j in range(1, 8):
         for copy in send_to_owner(j):
@@ -346,7 +312,7 @@
 
 
 def shards(queries, new_latent, cache, lengths, w_uk, w_uv):
-    anywhere = pl.BlockSpec(memory_space=pl.ANY)
+    anywhere = pl.BlockSpec(memory_space=pltpu.HBM)
     dma = pltpu.SemaphoreType.DMA
     return pl.pallas_call(
         kernel,
@@ -355,12 +321,13 @@
             anywhere,
             anywhere,
             anywhere,
-            pl.BlockSpec(memory_space=pltpu.SMEM),
+            anywhere,
             anywhere,
             anywhere,
         ],
         out_specs=pl.BlockSpec(memory_space=pltpu.VMEM),
         scratch_shapes=[
+            pltpu.SMEM((SEQS,), jnp.int32),
             pltpu.VMEM((GROUP * NOPE, LATENT), BF16),
             pltpu.VMEM((GROUP * LATENT, VDIM), BF16),
             pltpu.VMEM((GROUP, NOPE + ROPE), BF16),
@@ -377,7 +344,7 @@
             pltpu.VMEM((2, 2 * HEADS), F32),
             pltpu.VMEM((8, GROUP, LATENT), BF16),
             pltpu.VMEM((8, 2, 2 * HEADS), F32),
-            dma((5,)),
+            dma((6,)),
             dma((3,)),
             dma((4,)),
             dma((3,)),
@@ -394,20 +361,21 @@
             dma((8,)),
             dma((8,)),
             dma((8,)),
-            pltpu.SemaphoreType.REGULAR,
-            pltpu.SemaphoreType.REGULAR,
         ],
         compiler_params=pltpu.CompilerParams(
-            collective_id=0, has_side_effects=True, vmem_limit_bytes=67_043_328
+            collective_id=0, has_side_effects=True, vmem_limit_bytes=40 << 20
         ),
-    )(
-        queries,
-        new_latent,
-        jnp.swapaxes(cache, 1, 2),
-        lengths,
-        w_uk.reshape(GROUP * NOPE, LATENT),
-        w_uv.reshape(GROUP * LATENT, VDIM),
-    )
+    )(*[
+        pltpu.with_memory_space_constraint(array, pltpu.HBM)
+        for array in (
+            queries,
+            new_latent,
+            jnp.swapaxes(cache, 1, 2),
+            lengths,
+            w_uk.reshape(GROUP * NOPE, LATENT),
+            w_uv.reshape(GROUP * LATENT, VDIM),
+        )
+    ])
 
 
 def solution(mesh):

time: 41.8 us -> 39.4 us (0.943)
  Pallas kernels: 40.3 us -> 38.6 us
  local copies, waits for them, and re-layouts: 1.28 us -> 0.6 us
    pallas_call x1, Pallas kernels: 40.3 us -> 38.6 us  [shards(): pl.pallas_call(kernel, out_shape=jax.ShapeDtypeStruct((1, GROUP, VDIM), B...]
    unnamed x1, local copies, waits for them, and re-layouts: 1.28 us -> 0.6 us
where the time goes in v3:
time: 39.4 us; the launch traced here: 39.2 us
  Pallas kernels  38.6 us (98%)
  local copies, waits for them, and re-layouts  0.6 us (2%)
    pallas_call x1, Pallas kernels, shards(): pl.pallas_call(kernel, out_shape=jax.ShapeDtypeStruct((1, GROUP, VDIM), B...  38.6 us

profile of v3, /device:TPU:1, one launch (start us, length us, event | category | flops | bytes accessed | tf_op | source)
XLA Modules:
  0.0 39.2 jit_solution(9068224966020043672)
XLA Ops:
  0.0 38.6 %shard_map.64 = bf16[1,16,128]{2,1,0:T(8,128)(2,1)S(1)} custom-call(bf16[1,16,192]{2,1,0:T(8,128)(2,1)} %q_hbm.1, bf16[1,576]{1,0:T(2,128)(2,1)} %nl_hbm.1, bf16[4,576,128]{2,1,0:T(8,128)(2,1)} %bitcast.5, s32[16]{0:T(128)} %len_hbm.1, bf16[2048,512]{1,0:T(8,128)(2,1)} %bitcast.3, bf16[8192,128]{1,0:T(8,128)(2,1)} %bitcast.4), custom_call_target="tpu_custom_call" | custom-call | tf_op jit(solution)/shard_map/pallas_call | solution.py:317
  38.6 0.6 %copy.8 = bf16[1,16,128]{2,1,0:T(8,128)(2,1)} copy(bf16[1,16,128]{2,1,0:T(8,128)(2,1)S(1)} %shard_map.64) | data formatting | bytes 8192

commit v4 on v3

--- a/solution.py
+++ b/solution.py
@@ -16,6 +16,7 @@
 SEQS = 16
 SLOTS = 128
 NEG = -1e30
+PACKED = GROUP * WIDTH // 128
 SCALE = (NOPE + ROPE) ** -0.5
 MESH = pl.DeviceIdType.MESH
 F32 = jnp.float32
@@ -30,7 +31,7 @@
     q_hbm, nl_hbm, cache_hbm, len_hbm, wuk_hbm, wuv_hbm, out_ref,
     len_ref, wuk, wuv, q_in, nl, kt, kv, q_own, q_all, o_out, s_out, o_in, s_in,
     r_out, t_out, r_in, t_in,
-    local_sem, swap_send, swap_recv, nl_send, nl_recv, a_send, a_recv, b_send, b_recv,
+    local_sem, swap_send, swap_recv, nl_send, nl_recv, a_send, a_recv, f_send, b_send, b_recv,
     o_send, o_recv, s_send, s_recv, r_send, r_recv, t_send, t_recv,
 ):
     seq, head = lax.axis_index("seq"), lax.axis_index("head")
@@ -56,6 +57,8 @@
         return at(from_zhi, from_y, x, lax.rem(core + j // 4, 2)), lax.rem(head + j % 4, 4)
 
     odd = lax.rem(x, 2)
+    relays = (from_zhi != zhi) & (from_y == y)
+    along_y = [(at(zhi, lax.rem(y + d, 4), x, core), head) for d in (1, 3, 2)]
     near_x, pair_x, upper = x + 1 - 2 * odd, 3 - x, lax.div(x, 2)
     twin = (at(zhi, y, x, 1 - core), head)
     beside = (at(zhi, y, near_x, core), head)
@@ -76,7 +79,7 @@
         greet(worker(0))
         greet(owner(0))
 
-    for device in mates + pair:
+    for device in mates + pair + along_y:
         greet(device)
 
     def remote(src, dst, send, recv, device):
@@ -109,27 +112,29 @@
     q = q_in[...]
     row_of = lax.broadcasted_iota(jnp.int32, (GROUP, GROUP * NOPE), 0)
     col_of = lax.broadcasted_iota(jnp.int32, (GROUP, GROUP * NOPE), 1)
-    spread = jnp.concatenate([q[:, :NOPE].astype(F32)] * GROUP, axis=1)
-    spread = jnp.where(lax.div(col_of, NOPE) == row_of, spread, 0.0).astype(BF16)
+    diagonal = jnp.concatenate([q[:, :NOPE].astype(F32)] * GROUP, axis=1)
+    diagonal = jnp.where(lax.div(col_of, NOPE) == row_of, diagonal, 0.0).astype(BF16)
     load_wuk.wait()
-    absorbed = dot(spread, wuk[...], ((1,), (0,)))
-    q_own[:, :LATENT] = absorbed.astype(BF16)
-    q_own[:, LATENT:] = q[:, NOPE:]
-
-    pl.semaphore_wait(barrier, jnp.where(own_piece, 19, 21))
+    absorbed = dot(diagonal, wuk[...], ((1,), (0,)))
+    for i in range(4):
+        q_own[GROUP * i : GROUP * (i + 1)] = absorbed[:, 128 * i : 128 * (i + 1)].astype(BF16)
+    rope = q[:, NOPE:].astype(F32)
+    rope = jnp.concatenate([rope[: GROUP // 2], rope[GROUP // 2 :]], axis=1)
+    q_own[4 * GROUP :] = rope.astype(BF16)
+
+    pl.semaphore_wait(barrier, jnp.where(own_piece, 22, 24))
 
     my_slot = core * 4 + head
 
     def rows_of(x_, core_, head_):
-        start = pl.multiple_of(GROUP * head_, GROUP)
-        return q_all.at[2 * lax.rem(x_, 2) + core_, pl.ds(start, GROUP)]
+        return q_all.at[2 * lax.rem(x_, 2) + core_, head_]
 
     my_place = rows_of(x, core, head)
 
     def send_queries(j):
         return remote(q_own, my_place, a_send.at[j], a_recv.at[my_slot], worker(j))
 
-    for j in (4, 5, 7, 6, 1, 3, 2):
+    for j in (4, 1, 3, 2):
         send_queries(j).start()
 
     @pl.when(own_piece)
@@ -161,15 +166,30 @@
         place = rows_of(x, c, g)
         return remote(place, place, b_send.at[4 * c + g], b_recv.at[4 * c + g], beside)
 
-    for g in range(4):
+    def spread(c, g):
+        place = rows_of(x, c, g)
+        return [
+            remote(place, place, f_send.at[d, 4 * c + g], a_recv.at[4 * c + g], along_y[d])
+            for d in range(3)
+        ]
+
+    for k in range(4):
+        g = jnp.where(zhi == 0, k, 3 - k)
         for c in range(2):
             pltpu.make_async_copy(q_own, rows_of(x, c, g), a_recv.at[4 * c + g]).wait()
+
+            @pl.when(relays)
+            def _():
+                for copy in spread(c, g):
+                    copy.start()
+
             forward(c, g).start()
 
     load_kt.wait()
     for block in (1 - core, 2, 3):
         pltpu.make_async_copy(cache_hbm.at[0], slots(block), swap_recv.at[block]).wait()
-    kv[...] = kt[...].T
+    kv[:, :LATENT] = kt[:LATENT].T
+    kv[:, LATENT:] = jnp.concatenate([kt[LATENT:], kt[LATENT:]], axis=0).T
 
     chip = lax.div(seq, 2)
     load_len.wait()
@@ -177,7 +197,18 @@
     step = (3 - 2 * x) * (2 * SLOTS)
 
     def partial_of(x_):
-        queries = q_all[pl.ds(2 * lax.rem(x_, 2), 2)].reshape(2 * HEADS, WIDTH)
+        pieces = pl.ds(2 * lax.rem(x_, 2), 2)
+        queries = [
+            q_all[pieces, :, GROUP * i : GROUP * (i + 1)].reshape(2 * HEADS, 128)
+            for i in range(4)
+        ]
+        ropes = q_all[pieces, :, 4 * GROUP :].astype(F32)
+        first = lax.broadcasted_iota(jnp.int32, ropes.shape, 3) < ROPE
+        ropes = jnp.concatenate(
+            [jnp.where(first, ropes, 0.0), jnp.where(first, 0.0, ropes)], axis=2
+        )
+        queries.append(ropes.reshape(2 * HEADS, 128).astype(BF16))
+        queries = jnp.concatenate(queries, axis=1)
         scores = dot(kv[...], queries, ((1,), (1,))) * SCALE
         slot = lax.broadcasted_iota(jnp.int32, scores.shape, 0)
         position = chip * (2 * SLOTS) + jnp.where(
@@ -245,7 +276,8 @@
     for k in range(1, 4):
         other_token = lax.rem(token + k, SPEC)
         pltpu.make_async_copy(nl.at[token], nl.at[other_token], nl_recv.at[other_token]).wait()
-    mine = q_own[...].astype(F32)
+    mine = [q_own[GROUP * i : GROUP * (i + 1)].astype(F32) for i in range(4)]
+    mine = jnp.concatenate(mine + [q_in[:, NOPE:].astype(F32)], axis=1)
     fresh, keys = [], []
     for i in range(SPEC):
         key = nl[i].astype(F32)
@@ -294,9 +326,10 @@
     out_ref[0] = (projected[:GROUP] + projected[GROUP:]).astype(BF16)
 
     for j in range(1, 8):
-        send_queries(j).wait_send()
         for copy in send_to_owner(j):
             copy.wait_send()
+    for j in range(1, 5):
+        send_queries(j).wait_send()
 
     @pl.when(others_piece)
     def _():
@@ -307,6 +340,14 @@
     for g in range(4):
         for c in range(2):
             forward(c, g).wait_send()
+
+    @pl.when(relays)
+    def _():
+        for g in range(4):
+            for c in range(2):
+                for copy in spread(c, g):
+                    copy.wait_send()
+
     for copy in swaps + news + back:
         copy.wait_send()
 
@@ -333,9 +374,9 @@
             pltpu.VMEM((GROUP, NOPE + ROPE), BF16),
             pltpu.VMEM((SPEC, 1, WIDTH), BF16),
             pltpu.VMEM((WIDTH, 4 * SLOTS), BF16),
-            pltpu.VMEM((4 * SLOTS, WIDTH), BF16),
-            pltpu.VMEM((GROUP, WIDTH), BF16),
-            pltpu.VMEM((4, HEADS, WIDTH), BF16),
+            pltpu.VMEM((4 * SLOTS, LATENT + 128), BF16),
+            pltpu.VMEM((PACKED, 128), BF16),
+            pltpu.VMEM((4, 4, PACKED, 128), BF16),
             pltpu.VMEM((LATENT, 2 * HEADS), BF16),
             pltpu.VMEM((2, 2 * HEADS), F32),
             pltpu.VMEM((LATENT, 2 * HEADS), BF16),
@@ -351,6 +392,7 @@
             dma((4,)),
             dma((8,)),
             dma((8,)),
+            dma((3, 8)),
             dma((8,)),
             dma((8,)),
             dma,

time: 39.4 us -> 36.9 us (0.937)
  Pallas kernels: 38.6 us -> 36.2 us
    pallas_call x1, Pallas kernels: 38.6 us -> 36.2 us  [shards(): pl.pallas_call(kernel, out_shape=jax.ShapeDtypeStruct((1, GROUP, VDIM), B...]
where the time goes in v4:
time: 36.9 us; the launch traced here: 36.8 us
  Pallas kernels  36.2 us (98%)
  local copies, waits for them, and re-layouts  0.6 us (2%)
    pallas_call x1, Pallas kernels, shards(): pl.pallas_call(kernel, out_shape=jax.ShapeDtypeStruct((1, GROUP, VDIM), B...  36.2 us

profile of v4, /device:TPU:1, one launch (start us, length us, event | category | flops | bytes accessed | tf_op | source)
XLA Modules:
  0.0 36.8 jit_solution(7443173564290772301)
XLA Ops:
  0.0 36.2 %shard_map.64 = bf16[1,16,128]{2,1,0:T(8,128)(2,1)S(1)} custom-call(bf16[1,16,192]{2,1,0:T(8,128)(2,1)} %q_hbm.1, bf16[1,576]{1,0:T(2,128)(2,1)} %nl_hbm.1, bf16[4,576,128]{2,1,0:T(8,128)(2,1)} %bitcast.5, s32[16]{0:T(128)} %len_hbm.1, bf16[2048,512]{1,0:T(8,128)(2,1)} %bitcast.3, bf16[8192,128]{1,0:T(8,128)(2,1)} %bitcast.4), custom_call_target="tpu_custom_call" | custom-call | tf_op jit(solution)/shard_map/pallas_call | solution.py:358
  36.2 0.6 %copy.8 = bf16[1,16,128]{2,1,0:T(8,128)(2,1)} copy(bf16[1,16,128]{2,1,0:T(8,128)(2,1)S(1)} %shard_map.64) | data formatting | bytes 8192

commit v5 on v4

--- a/solution.py
+++ b/solution.py
@@ -13,6 +13,8 @@
 SPEC = 4
 GROUP = 16
 HEADS = 64
+PARTS = 2
+PART = LATENT // PARTS
 SEQS = 16
 SLOTS = 128
 NEG = -1e30
@@ -57,8 +59,11 @@
         return at(from_zhi, from_y, x, lax.rem(core + j // 4, 2)), lax.rem(head + j % 4, 4)
 
     odd = lax.rem(x, 2)
-    relays = (from_zhi != zhi) & (from_y == y)
-    along_y = [(at(zhi, lax.rem(y + d, 4), x, core), head) for d in (1, 3, 2)]
+    y_from = lax.rem(y + 4 - from_y, 4)
+    relays = (from_zhi != zhi) & (y_from == 0)
+    passes = (from_zhi != zhi) & (y_from == 3 - 2 * core)
+    along_y = [(at(zhi, lax.rem(y + d, 4), x, core), head) for d in (1, 3)]
+    onward_y = (at(zhi, lax.rem(y + 3 - 2 * core, 4), x, core), head)
     near_x, pair_x, upper = x + 1 - 2 * odd, 3 - x, lax.div(x, 2)
     twin = (at(zhi, y, x, 1 - core), head)
     beside = (at(zhi, y, near_x, core), head)
@@ -70,14 +75,14 @@
     def greet(device):
         pl.semaphore_signal(barrier, inc=1, device_id=device, device_id_type=MESH)
 
-    for j in range(7, 0, -1):
-        greet(worker(j))
-        greet(owner(j))
-
-    @pl.when(others_piece)
-    def _():
-        greet(worker(0))
-        greet(owner(0))
+    @pl.when((from_zhi == zhi) | (from_y == y))
+    def _():
+        for j in range(7, 0, -1):
+            greet(owner(j))
+
+        @pl.when(others_piece)
+        def _():
+            greet(owner(0))
 
     for device in mates + pair + along_y:
         greet(device)
@@ -122,7 +127,7 @@
     rope = jnp.concatenate([rope[: GROUP // 2], rope[GROUP // 2 :]], axis=1)
     q_own[4 * GROUP :] = rope.astype(BF16)
 
-    pl.semaphore_wait(barrier, jnp.where(own_piece, 22, 24))
+    pl.semaphore_wait(barrier, jnp.where(own_piece, 11, 12))
 
     my_slot = core * 4 + head
 
@@ -170,8 +175,14 @@
         place = rows_of(x, c, g)
         return [
             remote(place, place, f_send.at[d, 4 * c + g], a_recv.at[4 * c + g], along_y[d])
-            for d in range(3)
+            for d in range(2)
         ]
+
+    def pass_on(c, g):
+        place = rows_of(x, c, g)
+        return remote(
+            place, place, f_send.at[0, 4 * c + g], a_recv.at[4 * c + g], onward_y
+        )
 
     for k in range(4):
         g = jnp.where(zhi == 0, k, 3 - k)
@@ -182,6 +193,10 @@
             def _():
                 for copy in spread(c, g):
                     copy.start()
+
+            @pl.when(passes)
+            def _():
+                pass_on(c, g).start()
 
             forward(c, g).start()
 
@@ -218,60 +233,75 @@
         top = jnp.max(jnp.where(visible, scores, NEG), axis=0, keepdims=True)
         p = jnp.where(visible, jnp.exp(scores - top), 0.0)
         total = jnp.sum(p, axis=0, keepdims=True)
-        weighted = dot(kt[:LATENT], p.astype(BF16), ((1,), (0,)))
-        return top, total, weighted
+        return top, total, p.astype(BF16)
+
+    def weighted_of(p, j):
+        return dot(kt[PART * j : PART * (j + 1)], p, ((1,), (0,)))
 
     def put_stats(ref, top, total):
         ref[0:1] = top
         ref[1:2] = total
 
-    top_0, total_0, weighted_0 = partial_of(x)
-    for g in range(4):
+    for k in range(4):
         for c in range(2):
-            pltpu.make_async_copy(q_own, rows_of(near_x, c, g), b_recv.at[4 * c + g]).wait()
-    top_1, total_1, weighted_1 = partial_of(near_x)
-    o_out[...] = weighted_1.astype(BF16)
+            pltpu.make_async_copy(q_own, rows_of(near_x, c, k), b_recv.at[4 * c + k]).wait()
+    top_1, total_1, p_1 = partial_of(near_x)
     put_stats(s_out, top_1, total_1)
-    back = [
-        remote(s_out, s_in, s_send, s_recv, beside),
-        remote(o_out, o_in, o_send, o_recv, beside),
-    ]
-    for copy in back:
-        copy.start()
-
-    for copy in back:
-        copy.wait_recv()
+    back_s = remote(s_out, s_in, s_send, s_recv, beside)
+    back_s.start()
+    back = []
+    for j in range(PARTS):
+        o_out[j] = weighted_of(p_1, j).astype(BF16)
+        back.append(remote(o_out.at[j], o_in.at[j], o_send.at[j], o_recv.at[j], beside))
+        back[j].start()
+    top_0, total_0, p_0 = partial_of(x)
+    weighted_0 = [weighted_of(p_0, j) for j in range(PARTS)]
+
+    back_s.wait_recv()
     top_1, total_1 = s_in[0:1], s_in[1:2]
     top = jnp.maximum(top_0, top_1)
     factor_0, factor_1 = jnp.exp(top_0 - top), jnp.exp(top_1 - top)
     put_stats(t_out, top, total_0 * factor_0 + total_1 * factor_1)
-    merged = weighted_0 * factor_0 + o_in[...].astype(F32) * factor_1
-    r_out[...] = merged.T.astype(BF16)
-
-    def piece(j):
+
+    def place_of(j):
         core_, head_ = lax.rem(core + j // 4, 2), lax.rem(head + j % 4, 4)
-        start = pl.multiple_of(HEADS * core_ + GROUP * head_, GROUP)
-        return r_out.at[pl.ds(start, GROUP)]
-
-    def send_to_owner(j):
-        return (
-            remote(t_out, t_in.at[plane], t_send.at[j], t_recv.at[plane], owner(j)),
-            remote(piece(j), r_in.at[plane], r_send.at[j], r_recv.at[plane], owner(j)),
-        )
-
-    for j in range(1, 8):
-        for copy in send_to_owner(j):
-            copy.start()
-
-    @pl.when(own_piece)
-    def _():
-        pltpu.make_async_copy(t_out, t_in.at[plane], t_recv.at[plane]).start()
-        pltpu.make_async_copy(piece(0), r_in.at[plane], r_recv.at[plane]).start()
-
-    @pl.when(others_piece)
-    def _():
-        for copy in send_to_owner(0):
-            copy.start()
+        return pl.ds(pl.multiple_of(HEADS * core_ + GROUP * head_, GROUP), GROUP)
+
+    def send_stats(j):
+        return remote(t_out, t_in.at[plane], t_send.at[j], t_recv.at[plane], owner(j))
+
+    def send_part(j, i):
+        return remote(
+            r_out.at[i, place_of(j)], r_in.at[plane, i], r_send.at[j, i],
+            r_recv.at[plane, i], owner(j),
+        )
+
+    def to_owners(send, keep):
+        for j in range(7, 0, -1):
+            send(j).start()
+
+        @pl.when(own_piece)
+        def _():
+            keep().start()
+
+        @pl.when(others_piece)
+        def _():
+            send(0).start()
+
+    to_owners(
+        send_stats,
+        lambda: pltpu.make_async_copy(t_out, t_in.at[plane], t_recv.at[plane]),
+    )
+    for i in range(PARTS):
+        back[i].wait_recv()
+        merged = weighted_0[i] * factor_0 + o_in[i].astype(F32) * factor_1
+        r_out[i] = merged.T.astype(BF16)
+        to_owners(
+            lambda j, i=i: send_part(j, i),
+            lambda i=i: pltpu.make_async_copy(
+                r_out.at[i, place_of(0)], r_in.at[plane, i], r_recv.at[plane, i]
+            ),
+        )
 
     for k in range(1, 4):
         other_token = lax.rem(token + k, SPEC)
@@ -294,7 +324,8 @@
 
     for k in range(8):
         pltpu.make_async_copy(t_in.at[k], t_in.at[k], t_recv.at[k]).wait()
-        pltpu.make_async_copy(r_in.at[k], r_in.at[k], r_recv.at[k]).wait()
+        for i in range(PARTS):
+            pltpu.make_async_copy(r_in.at[k, i], r_in.at[k, i], r_recv.at[k, i]).wait()
     lane = lax.broadcasted_iota(jnp.int32, (GROUP, 2 * HEADS), 1)
     mine_lane = lane == (
         HEADS * core + GROUP * head + lax.broadcasted_iota(jnp.int32, (GROUP, 2 * HEADS), 0)
@@ -313,7 +344,8 @@
     for k in range(8):
         factor = jnp.exp(tops[k] - top)
         total = total + column(t_in[k, 1:2]) * factor
-        latent = latent + r_in[k].astype(F32) * factor
+        parts = jnp.concatenate([r_in[k, i] for i in range(PARTS)], axis=1)
+        latent = latent + parts.astype(F32) * factor
     latent = latent / total
 
     high = latent.astype(BF16).astype(F32)
@@ -326,16 +358,18 @@
     out_ref[0] = (projected[:GROUP] + projected[GROUP:]).astype(BF16)
 
     for j in range(1, 8):
-        for copy in send_to_owner(j):
-            copy.wait_send()
+        send_stats(j).wait_send()
+        for i in range(PARTS):
+            send_part(j, i).wait_send()
     for j in range(1, 5):
         send_queries(j).wait_send()
 
     @pl.when(others_piece)
     def _():
         send_queries(0).wait_send()
-        for copy in send_to_owner(0):
-            copy.wait_send()
+        send_stats(0).wait_send()
+        for i in range(PARTS):
+            send_part(0, i).wait_send()
 
     for g in range(4):
         for c in range(2):
@@ -348,7 +382,13 @@
                 for copy in spread(c, g):
                     copy.wait_send()
 
-    for copy in swaps + news + back:
+    @pl.when(passes)
+    def _():
+        for g in range(4):
+            for c in range(2):
+                pass_on(c, g).wait_send()
+
+    for copy in swaps + news + back + [back_s]:
         copy.wait_send()
 
 
@@ -377,13 +417,13 @@
             pltpu.VMEM((4 * SLOTS, LATENT + 128), BF16),
             pltpu.VMEM((PACKED, 128), BF16),
             pltpu.VMEM((4, 4, PACKED, 128), BF16),
-            pltpu.VMEM((LATENT, 2 * HEADS), BF16),
+            pltpu.VMEM((PARTS, PART, 2 * HEADS), BF16),
             pltpu.VMEM((2, 2 * HEADS), F32),
-            pltpu.VMEM((LATENT, 2 * HEADS), BF16),
+            pltpu.VMEM((PARTS, PART, 2 * HEADS), BF16),
             pltpu.VMEM((2, 2 * HEADS), F32),
-            pltpu.VMEM((2 * HEADS, LATENT), BF16),
+            pltpu.VMEM((PARTS, 2 * HEADS, PART), BF16),
             pltpu.VMEM((2, 2 * HEADS), F32),
-            pltpu.VMEM((8, GROUP, LATENT), BF16),
+            pltpu.VMEM((8, PARTS, GROUP, PART), BF16),
             pltpu.VMEM((8, 2, 2 * HEADS), F32),
             dma((6,)),
             dma((3,)),
@@ -392,15 +432,15 @@
             dma((4,)),
             dma((8,)),
             dma((8,)),
-            dma((3, 8)),
-            dma((8,)),
-            dma((8,)),
+            dma((2, 8)),
+            dma((8,)),
+            dma((8,)),
+            dma((PARTS,)),
+            dma((PARTS,)),
             dma,
             dma,
-            dma,
-            dma,
-            dma((8,)),
-            dma((8,)),
+            dma((8, PARTS)),
+            dma((8, PARTS)),
             dma((8,)),
             dma((8,)),
         ],

time: 36.9 us -> 35.2 us (0.954)
  Pallas kernels: 36.2 us -> 34.5 us
    pallas_call x1, Pallas kernels: 36.2 us -> 34.5 us  [shards(): pl.pallas_call(kernel, out_shape=jax.ShapeDtypeStruct((1, GROUP, VDIM), B...]
where the time goes in v5:
time: 35.2 us; the launch traced here: 35.1 us
  Pallas kernels  34.5 us (98%)
  local copies, waits for them, and re-layouts  0.6 us (2%)
    pallas_call x1, Pallas kernels, shards(): pl.pallas_call(kernel, out_shape=jax.ShapeDtypeStruct((1, GROUP, VDIM), B...  34.5 us

profile of v5, /device:TPU:1, one launch (start us, length us, event | category | flops | bytes accessed | tf_op | source)
XLA Modules:
  0.0 35.1 jit_solution(11396323726144217099)
XLA Ops:
  0.0 34.5 %shard_map.64 = bf16[1,16,128]{2,1,0:T(8,128)(2,1)S(1)} custom-call(bf16[1,16,192]{2,1,0:T(8,128)(2,1)} %q_hbm.1, bf16[1,576]{1,0:T(2,128)(2,1)} %nl_hbm.1, bf16[4,576,128]{2,1,0:T(8,128)(2,1)} %bitcast.5, s32[16]{0:T(128)} %len_hbm.1, bf16[2048,512]{1,0:T(8,128)(2,1)} %bitcast.3, bf16[8192,128]{1,0:T(8,128)(2,1)} %bitcast.4), custom_call_target="tpu_custom_call" | custom-call | tf_op jit(solution)/shard_map/pallas_call | solution.py:398
  34.5 0.6 %copy.8 = bf16[1,16,128]{2,1,0:T(8,128)(2,1)} copy(bf16[1,16,128]{2,1,0:T(8,128)(2,1)S(1)} %shard_map.64) | data formatting | bytes 8192

commit v6 on v5

--- a/solution.py
+++ b/solution.py
@@ -59,11 +59,8 @@
         return at(from_zhi, from_y, x, lax.rem(core + j // 4, 2)), lax.rem(head + j % 4, 4)
 
     odd = lax.rem(x, 2)
-    y_from = lax.rem(y + 4 - from_y, 4)
-    relays = (from_zhi != zhi) & (y_from == 0)
-    passes = (from_zhi != zhi) & (y_from == 3 - 2 * core)
-    along_y = [(at(zhi, lax.rem(y + d, 4), x, core), head) for d in (1, 3)]
-    onward_y = (at(zhi, lax.rem(y + 3 - 2 * core, 4), x, core), head)
+    relays = (from_zhi != zhi) & (from_y == y)
+    along_y = [(at(zhi, lax.rem(y + d, 4), x, core), head) for d in (2, 1, 3)]
     near_x, pair_x, upper = x + 1 - 2 * odd, 3 - x, lax.div(x, 2)
     twin = (at(zhi, y, x, 1 - core), head)
     beside = (at(zhi, y, near_x, core), head)
@@ -127,7 +124,7 @@
     rope = jnp.concatenate([rope[: GROUP // 2], rope[GROUP // 2 :]], axis=1)
     q_own[4 * GROUP :] = rope.astype(BF16)
 
-    pl.semaphore_wait(barrier, jnp.where(own_piece, 11, 12))
+    pl.semaphore_wait(barrier, jnp.where(own_piece, 12, 13))
 
     my_slot = core * 4 + head
 
@@ -175,14 +172,8 @@
         place = rows_of(x, c, g)
         return [
             remote(place, place, f_send.at[d, 4 * c + g], a_recv.at[4 * c + g], along_y[d])
-            for d in range(2)
+            for d in range(3)
         ]
-
-    def pass_on(c, g):
-        place = rows_of(x, c, g)
-        return remote(
-            place, place, f_send.at[0, 4 * c + g], a_recv.at[4 * c + g], onward_y
-        )
 
     for k in range(4):
         g = jnp.where(zhi == 0, k, 3 - k)
@@ -193,10 +184,6 @@
             def _():
                 for copy in spread(c, g):
                     copy.start()
-
-            @pl.when(passes)
-            def _():
-                pass_on(c, g).start()
 
             forward(c, g).start()
 
@@ -381,12 +368,6 @@
             for c in range(2):
                 for copy in spread(c, g):
                     copy.wait_send()
-
-    @pl.when(passes)
-    def _():
-        for g in range(4):
-            for c in range(2):
-                pass_on(c, g).wait_send()
 
     for copy in swaps + news + back + [back_s]:
         copy.wait_send()
@@ -432,7 +413,7 @@
             dma((4,)),
             dma((8,)),
             dma((8,)),
-            dma((2, 8)),
+            dma((3, 8)),
             dma((8,)),
             dma((8,)),
             dma((PARTS,)),

time: 35.2 us -> 33 us (0.937)
  Pallas kernels: 34.5 us -> 32.3 us
    pallas_call x1, Pallas kernels: 34.5 us -> 32.3 us  [shards(): pl.pallas_call(kernel, out_shape=jax.ShapeDtypeStruct((1, GROUP, VDIM), B...]
where the time goes in v6:
time: 33 us; the launch traced here: 32.9 us
  Pallas kernels  32.3 us (98%)
  local copies, waits for them, and re-layouts  0.6 us (2%)
    pallas_call x1, Pallas kernels, shards(): pl.pallas_call(kernel, out_shape=jax.ShapeDtypeStruct((1, GROUP, VDIM), B...  32.3 us

profile of v6, /device:TPU:1, one launch (start us, length us, event | category | flops | bytes accessed | tf_op | source)
XLA Modules:
  0.0 32.9 jit_solution(13999048041759249757)
XLA Ops:
  0.0 32.3 %shard_map.64 = bf16[1,16,128]{2,1,0:T(8,128)(2,1)S(1)} custom-call(bf16[1,16,192]{2,1,0:T(8,128)(2,1)} %q_hbm.1, bf16[1,576]{1,0:T(2,128)(2,1)} %nl_hbm.1, bf16[4,576,128]{2,1,0:T(8,128)(2,1)} %bitcast.5, s32[16]{0:T(128)} %len_hbm.1, bf16[2048,512]{1,0:T(8,128)(2,1)} %bitcast.3, bf16[8192,128]{1,0:T(8,128)(2,1)} %bitcast.4), custom_call_target="tpu_custom_call" | custom-call | tf_op jit(solution)/shard_map/pallas_call | solution.py:379
  32.3 0.6 %copy.8 = bf16[1,16,128]{2,1,0:T(8,128)(2,1)} copy(bf16[1,16,128]{2,1,0:T(8,128)(2,1)S(1)} %shard_map.64) | data formatting | bytes 8192
